TPU v7x, 32 devices: a whole 2x2x4 slice. The times are simulated.
32 devices in a mesh: tile: 8 (over z, x), depth: 4 (over y, core).
Axes of the slice: x: 2, y: 2, z: 4, core: 2. Of those that a mesh axis runs over, the one named last changes fastest.
Arguments:
- density: float32 [64, 128, 128], P('depth', 'tile'), may hold values from 0.5 to 2
- momentum: float32 [3, 64, 128, 128], P(None, 'depth', 'tile'), may hold values from -4 to 4
- magnetic: float32 [3, 64, 128, 128], P(None, 'depth', 'tile'), may hold values from -4 to 4
- energy: float32 [64, 128, 128], P('depth', 'tile'), may hold values from 2 to 4
- shifts: int32 [24], replicated, may hold values from 0 to 55, as said below
- levels: int32 [24], replicated, may hold values from 0 to 63, as said below
Outputs:
- new_state: float32 [8, 64, 128, 128], P(None, 'depth', 'tile')
- intensity: float32 [48, 128, 128], P(None, 'tile', 'depth')
Inputs may be any that keep to these rules, and one draw needn't show every extreme that they name: shifts[k] = (1732 (levels[k] - levels[0]) + 1000) // 2000, the nearest whole column to tan(60 degrees) times the depth gap at half a column per level; the last is exactly 55. 24 distinct levels in ascending order, the first 0 and the last 63; each depth slab of 16 consecutive levels holds at most 8 of them, and some slab exactly 8.
All inputs are finite; a program needn't handle non-finite values.
Results may differ from a plain program's by a relative error of at most 0.000054.
Values sent between devices are 32-bit elements; how exact they have to be, the bound alone decides.
A program may use at most 64 MiB of HBM per device.

v0:
```python
import jax
import jax.numpy as jnp
from jax import lax
from jax.sharding import PartitionSpec as P

W = 48


GAMMA = 5.0 / 3.0
SECTION = 0.02
GRAVITY = 0.5
SIN_VIEW = 0.8660254037844386
COS_VIEW = 0.5
STRENGTH = 4.0
SPACING = 0.25


def shifted(block, axis, distance):
    devices = range(lax.axis_size(axis))
    route = [((i - distance) % len(devices), i) for i in devices]
    return lax.ppermute(block, axis, route)


def padded_2(cells, sides, width, closed):
    for axis, dim in sides:
        count = lax.axis_size(axis)
        ends = count if closed else count - 1
        head = lax.slice_in_dim(cells, 0, width, axis=dim)
        tail = lax.slice_in_dim(cells, cells.shape[dim] - width, cells.shape[dim], axis=dim)
        cells = jnp.concatenate(
            [
                lax.ppermute(tail, axis, [(i, (i + 1) % count) for i in range(ends)]),
                cells,
                lax.ppermute(head, axis, [((i + 1) % count, i) for i in range(ends)]),
            ],
            axis=dim,
        )
    return cells


def derive(padded, axis, count):

    def layer(offset):
        return lax.slice_in_dim(padded, offset, offset + count, axis=axis)

    return (
        45.0 * (layer(4) - layer(2)) - 9.0 * (layer(5) - layer(1)) + (layer(6) - layer(0))
    ) / 60.0


def flux(state, comp):
    rho = state[0]
    moment = state[1:4]
    field = state[4:7]
    energy = state[7]
    velocity = moment / rho
    field_sq = jnp.sum(field * field, axis=0)
    pressure = (GAMMA - 1.0) * (energy - 0.5 * jnp.sum(moment * velocity, axis=0) - 0.5 * field_sq)
    total = pressure + 0.5 * field_sq
    along = velocity[comp]
    normal = field[comp]
    flux_mom = (moment * along - field * normal).at[comp].add(total)
    flux_mag = along * field - normal * velocity
    flux_energy = (energy + total) * along - normal * jnp.sum(velocity * field, axis=0)
    return jnp.concatenate([moment[comp][None], flux_mom, flux_mag, flux_energy[None]], axis=0)


def tendency(along_x, along_y, along_z, state):
    depth_cells, width_cells, cross_cells = (state.shape[1], state.shape[2], state.shape[3])
    rate = -(
        derive(flux(along_x, 0), 2, width_cells)
        + derive(flux(along_y, 1), 3, cross_cells)
        + derive(flux(along_z, 2), 1, depth_cells)
    )
    rate = rate.at[3].add(GRAVITY * state[0])
    rate = rate.at[7].add(GRAVITY * state[3])
    return rate


def line_fields(new_state):
    dens = 0.5 + jax.nn.softplus(new_state[0])
    speed = (COS_VIEW * new_state[3] + SIN_VIEW * new_state[1]) / dens
    field_sq = jnp.sum(new_state[4:7] * new_state[4:7], axis=0)
    source = jax.nn.softplus(new_state[7] - 0.5 * field_sq) / dens
    return jnp.stack([dens, speed, source], axis=1)


def rows_mask(flags):
    return flags[:, None, None, None]


def shear(rows, row_shift, reach):
    cells = rows.shape[2]
    tiles_ahead = row_shift // cells
    offset = row_shift % cells

    def advance(turn, carry):
        piece, near, beyond = carry
        piece = shifted(piece, "tile", -1)
        near = jnp.where(rows_mask(tiles_ahead == turn), piece, near)
        beyond = jnp.where(rows_mask(tiles_ahead + 1 == turn), piece, beyond)
        return (piece, near, beyond)

    start_near = jnp.where(rows_mask(tiles_ahead == 0), rows, jnp.zeros_like(rows))
    carry = lax.fori_loop(1, reach + 2, advance, (rows, start_near, jnp.zeros_like(rows)))
    near = carry[1]
    beyond = carry[2]
    joined = jnp.concatenate([near, beyond], axis=2)
    target = jnp.arange(cells, dtype=jnp.int32)
    anchor = jnp.arange(2 * cells, dtype=jnp.int32)
    select = (anchor[None, None, :] == target[None, :, None] + offset[:, None, None]).astype(
        jnp.float32
    )
    return jnp.einsum("lcxa,lwx->lcwa", joined, select, precision=lax.Precision.HIGHEST)


def regroup(rows):
    return lax.all_to_all(rows, "depth", split_axis=3, concat_axis=0, tiled=True)


def emergent(columns):
    positions = columns.shape[0]
    flat = columns.reshape(positions, 3, -1)
    dens = flat[:, 0]
    speed = flat[:, 1]
    source = flat[:, 2]
    waves = (jnp.arange(W, dtype=jnp.float32) - 0.5 * (W - 1)) * SPACING
    gap = waves[:, None, None] - speed[None]
    dtau = 2.0 / positions * dens[None] * (1.0 + STRENGTH * jnp.exp(-gap * gap))
    order = jnp.arange(positions, dtype=jnp.int32)
    earlier = (order[None, :] < order[:, None]).astype(jnp.float32)
    above = jnp.einsum("kj,wjc->wkc", earlier, dtau, precision=lax.Precision.HIGHEST)
    inner = jnp.sum(source[None] * jnp.exp(-above) * (1.0 - jnp.exp(-dtau)), axis=1)
    total = inner + source[-1][None] * jnp.exp(-above[:, -1] - dtau[:, -1])
    return total.reshape((W,) + columns.shape[2:])


def per_device(density, momentum, magnetic, energy, shifts, levels):
    state = jnp.concatenate([density[None], momentum, magnetic, energy[None]], axis=0)
    count_vars, depth_cells, width_cells, cross_cells = state.shape
    depth_at = lax.axis_index("depth")
    slabs = lax.axis_size("depth")
    along_x = padded_2(state, (("tile", 2),), 3, True)
    padded = padded_2(state, (("depth", 1),), 3, False)
    rim_shape = (count_vars, 3, width_cells, cross_cells)
    head = jnp.where(depth_at == 0, jnp.broadcast_to(state[:, :1], rim_shape), padded[:, :3])
    tail = jnp.where(
        depth_at == slabs - 1,
        jnp.broadcast_to(state[:, -1:], rim_shape),
        padded[:, depth_cells + 3 :],
    )
    along_z = jnp.concatenate([head, state, tail], axis=1)
    along_y = jnp.pad(state, ((0, 0), (0, 0), (0, 0), (3, 3)), mode="wrap")
    new_state = state + SECTION * tendency(along_x, along_y, along_z, state)
    fields = line_fields(new_state)
    largest = (1732 * (depth_cells * slabs - 1) + 1000) // 2000
    reach = largest // width_cells
    lowest = depth_at * depth_cells
    local_level = lowest + jnp.arange(depth_cells, dtype=jnp.int32)
    match = local_level[:, None] == levels[None, :]
    level_shift = jnp.sum(jnp.where(match, shifts[None, :], 0), axis=1)
    columns = regroup(shear(fields, level_shift, reach))[levels]
    intensity = emergent(columns)
    return (new_state, intensity)


def solution(mesh):
    return jax.shard_map(
        per_device,
        mesh=mesh,
        in_specs=(
            P("depth", "tile", None),
            P(None, "depth", "tile", None),
            P(None, "depth", "tile", None),
            P("depth", "tile", None),
            P(),
            P(),
        ),
        out_specs=(P(None, "depth", "tile", None), P(None, "tile", "depth")),
        check_vma=False,
    )
```

profile of v0, /device:TPU:27, one launch (start us, length us, event | category | flops | bytes accessed | tf_op | source)
XLA Modules:
  0.0 124.2 jit_solution(16690774001178542910)
XLA Ops:
  0.6 1.3 %pad_maximum_fusion.4 = f32[8,16,16,128]{3,2,1,0:T(8,128)S(1)} fusion(f32[1,16,16,128]{3,2,1,0:T(8,128)} %bitcast.161, f32[3,16,16,128]{3,2,1,0:T(8,128)} %param.20, f32[3,16,16,128]{3,2,1,0:T(8,128)} %param.19, f32[1,16,16,128]{3,2,1,0:T(8,128)} %bitcast.147), kind=kLoop, calls=%fused_computation.76 | loop fusion | flops 786432 | bytes 2097152 | tf_op jit(solution)/shard_map/concatenate | solution.py:139
  1.9 0.8 fusion.81
  2.7 2.6 %collective-permute-start.4 = (f32[8,3,16,128]{3,2,1,0:T(8,128)}, f32[8,3,16,128]{3,2,1,0:T(8,128)}, u32[]{:S(2)}, u32[]{:S(2)}) collective-permute-start(f32[8,3,16,128]{3,2,1,0:T(8,128)} %get-tuple-element.273), channel_id=1, source_target_pairs={{1,0},{2,1},{3,2},{5,4},{6,5},{7,6},{9,8},{10,9},{11,10},{13,12},{... | collective-permute-start | bytes 589832 | tf_op jit(solution)/shard_map/ppermute | solution.py:34
  5.3 3.0 %collective-permute-start.3 = (f32[8,3,16,128]{3,2,1,0:T(8,128)}, f32[8,3,16,128]{3,2,1,0:T(8,128)}, u32[]{:S(2)}, u32[]{:S(2)}) collective-permute-start(f32[8,3,16,128]{3,2,1,0:T(8,128)} %get-tuple-element.272), channel_id=1, source_target_pairs={{0,1},{1,2},{2,3},{4,5},{5,6},{6,7},{8,9},{9,10},{10,11},{12,13},{... | collective-permute-start | bytes 589832 | tf_op jit(solution)/shard_map/ppermute | solution.py:32
  8.4 0.9 fusion.79
  9.3 0.3 collective-permute-start.2
  9.5 3.9 %collective-permute-start.1 = (f32[8,16,3,128]{3,2,1,0:T(4,128)}, f32[8,16,3,128]{3,2,1,0:T(4,128)}, u32[]{:S(2)}, u32[]{:S(2)}) collective-permute-start(f32[8,16,3,128]{3,2,1,0:T(4,128)} %get-tuple-element.266), channel_id=1, source_target_pairs={{0,4},{4,8},{8,12},{12,16},{16,20},{20,24},{24,28},{28,0},{1,5},{5... | collective-permute-start | bytes 589832 | tf_op jit(solution)/shard_map/ppermute | solution.py:32
  13.5 0.7 slice_bitcast_fusion.6
  14.1 0.3 fusion.80
  14.5 0.6 copy-done
  15.3 1.1 maximum_bitcast_fusion
  16.3 2.2 %pad_maximum_fusion = f32[8,16,16,134]{3,2,1,0:T(8,128)} fusion(f32[8,16,16,3]{3,2,1,0:T(8,128)S(1)} %get-tuple-element.269, f32[1,16,16,128]{3,2,1,0:T(8,128)S(1)} %bitcast.163, f32[3,16,16,128]{3,2,1,0:T(8,128)S(1)} %copy-done.1, f32[3,16,16,128]{3,2,1,0:T(8,128)S(1)} %copy-done, f32[1,16,16,128]{3,2,1,0:T(8,128)S(1)} %bitcast.149, ...), kind=kLoop, calls=%fused_computation.23 | loop fusion | flops 1372160 | bytes 2195456 | tf_op jit(solution)/shard_map/jit(_pad)/concatenate | solution.py:153
  18.6 0.6 add_multiply_fusion
  19.2 3.5 %multiply_reduce_fusion.3 = (f32[16,16,134]{2,1,0:T(8,128)}, f32[16,16,134]{2,1,0:T(8,128)}, f32[16,16,134]{2,1,0:T(8,128)}, f32[3,16,16,134]{3,2,1,0:T(8,128)}) fusion(f32[8,16,16,134]{3,2,1,0:T(8,128)} %pad_maximum_fusion, f32[16,16,134]{2,1,0:T(8,128)} %get-tuple-element.251), kind=kLoop, calls=%fused_computation.84 | loop fusion | flops 617472 | bytes 1783808 | tf_op jit(solution)/shard_map/reduce_sum | solution.py:58
  22.7 1.7 %slice_bitcast_fusion = f32[16,16,134]{2,1,0:T(8,128)} fusion(f32[3,16,16,134]{3,2,1,0:T(8,128)} %get-tuple-element.243), kind=kLoop, calls=%fused_computation.116 | loop fusion | bytes 274432 | tf_op jit(solution)/shard_map/mul | solution.py:62
  24.6 2.1 %multiply_subtract_fusion = (f32[3,16,16,134]{3,2,1,0:T(8,128)S(1)}, f32[3,16,16,134]{3,2,1,0:T(8,128)S(1)}) fusion(f32[3,16,16,134]{3,2,1,0:T(8,128)} %get-tuple-element.243, f32[8,16,16,134]{3,2,1,0:T(8,128)} %pad_maximum_fusion, f32[16,16,134]{2,1,0:T(8,128)} %bitcast.178, f32[16,16,134]{2,1,0:T(8,128)} %slice_bitcast_fusion), kind=kLoop, calls=%fused_computation.82 | loop fusion | flops 617472 | bytes 2332672 | tf_op jit(solution)/shard_map/sub | solution.py:63
  26.8 0.3 fusion.50
  27.1 0.7 copy-done.5
  27.8 1.1 fusion.51
  28.9 0.3 fusion.6
  29.3 0.5 copy-done.10
  29.8 0.9 broadcast_select_fusion.2
  30.7 1.0 broadcast_select_fusion.3
  32.0 0.9 maximum_bitcast_fusion.1
  32.9 1.3 %pad_maximum_fusion.1 = f32[8,16,22,128]{3,2,1,0:T(8,128)S(1)} fusion(f32[8,16,3,128]{3,2,1,0:T(4,128)} %collective-permute-done.2, f32[1,16,16,128]{3,2,1,0:T(8,128)S(1)} %bitcast.169, f32[3,16,16,128]{3,2,1,0:T(8,128)S(1)} %copy-done.1, f32[3,16,16,128]{3,2,1,0:T(8,128)S(1)} %copy-done, f32[1,16,16,128]{3,2,1,0:T(8,128)S(1)} %bitcast.155, ...), kind=kLoop, calls=%fused_computation.37 | loop fusion | flops 1802240 | bytes 2883584 | tf_op jit(solution)/shard_map/concatenate | solution.py:30
  34.9 0.9 fusion.53
  36.0 1.2 fusion.15
  37.2 1.6 %fusion.33 = f32[8,16,16,128]{3,2,1,0:T(8,128)S(1)} fusion(f32[8,22,16,128]{3,2,1,0:T(8,128)S(1)} %fusion.24, f32[8,16,16,134]{3,2,1,0:T(8,128)S(1)} %fusion.6, f32[8,16,22,128]{3,2,1,0:T(8,128)S(1)} %fusion.15), kind=kLoop, calls=%fused_computation.55 | loop fusion | flops 6553600 | bytes 19922944 | tf_op jit(solution)/shard_map/neg | solution.py:70
  39.4 0.6 copy-done.4
  40.0 50.7 %while.23 = (s32[]{:T(128)}, f32[16,3,16,128]{3,2,1,0:T(8,128)S(1)}, f32[16,3,16,128]{3,2,1,0:T(8,128)S(1)}, f32[16,3,16,128]{3,2,1,0:T(8,128)S(1)}, s32[16]{0:T(128)S(1)}, /*index=5*/s32[]{:T(128)}, s32[]{:T(128)}) while((s32[]{:T(128)}, f32[16,3,16,128]{3,2,1,0:T(8,128)S(1)}, f32[16,3,16,128]{3,2,1,0:T(8,128)S(1)}, ...), condition=%wide.region_12.13_spmd.clone, body=%wide.region_11.12_spmd.clone.sunk | while | flops 294963 | bytes 4325643 | solution.py:105
  40.1 13.7 %collective-permute-done = f32[16,3,16,128]{3,2,1,0:T(8,128)S(1)} collective-permute-done((f32[16,3,16,128]{3,2,1,0:T(8,128)S(1)}, f32[16,3,16,128]{3,2,1,0:T(8,128)S(1)}, u32[]{:S(2)}, u32[]{:S(2)}) %collective-permute-start) | collective-permute-done | bytes 393248 | tf_op jit(solution)/shard_map/while/body/eval_jaxpr/ppermute | solution.py:21
  54.1 12.8 %collective-permute-done = f32[16,3,16,128]{3,2,1,0:T(8,128)S(1)} collective-permute-done((f32[16,3,16,128]{3,2,1,0:T(8,128)S(1)}, f32[16,3,16,128]{3,2,1,0:T(8,128)S(1)}, u32[]{:S(2)}, u32[]{:S(2)}) %collective-permute-start) | collective-permute-done | bytes 393248 | tf_op jit(solution)/shard_map/while/body/eval_jaxpr/ppermute | solution.py:21
  67.2 11.9 %collective-permute-done = f32[16,3,16,128]{3,2,1,0:T(8,128)S(1)} collective-permute-done((f32[16,3,16,128]{3,2,1,0:T(8,128)S(1)}, f32[16,3,16,128]{3,2,1,0:T(8,128)S(1)}, u32[]{:S(2)}, u32[]{:S(2)}) %collective-permute-start) | collective-permute-done | bytes 393248 | tf_op jit(solution)/shard_map/while/body/eval_jaxpr/ppermute | solution.py:21
  79.4 11.1 %collective-permute-done = f32[16,3,16,128]{3,2,1,0:T(8,128)S(1)} collective-permute-done((f32[16,3,16,128]{3,2,1,0:T(8,128)S(1)}, f32[16,3,16,128]{3,2,1,0:T(8,128)S(1)}, u32[]{:S(2)}, u32[]{:S(2)}) %collective-permute-start) | collective-permute-done | bytes 393248 | tf_op jit(solution)/shard_map/while/body/eval_jaxpr/ppermute | solution.py:21
  90.7 1.2 convolution_bitcast_fusion.1
  91.9 2.1 %copy.37 = f32[16,3,16,128]{2,0,1,3:T(8,128)S(1)} copy(f32[16,3,16,128]{3,2,1,0:T(8,128)} %convolution_bitcast_fusion.1) | data formatting | bytes 786432 | tf_op jit(solution)/shard_map/lcxa,lwx->lcwa/transpose | solution.py:114
  94.0 1.8 %reshape.515 = f32[4,1,24576]{2,1,0:T(1,128)} reshape(f32[128,3,16,16]{3,2,1,0:T(8,128)S(1)} %bitcast.175) | data formatting | bytes 786432
  95.8 6.5 %all-to-all-start = ((f32[4,1,24576]{2,1,0:T(1,128)}), f32[4,1,24576]{2,1,0:T(1,128)S(1)}, u32[]{:S(2)}, u32[]{:S(2)}) async-start(f32[4,1,24576]{2,1,0:T(1,128)} %reshape.515), calls=%async_computation | async-start | bytes 786432 | tf_op jit(solution)/shard_map/all_to_all | solution.py:118
  102.4 6.4 %all-to-all-done = f32[4,1,24576]{2,1,0:T(1,128)S(1)} async-done(((f32[4,1,24576]{2,1,0:T(1,128)}), f32[4,1,24576]{2,1,0:T(1,128)S(1)}, u32[]{:S(2)}, u32[]{:S(2)}) %all-to-all-start) | async-done | bytes 393248 | tf_op jit(solution)/shard_map/all_to_all | solution.py:118
  108.8 0.5 broadcast.492
  109.3 1.8 %reduce.16 = f32[4,24576]{1,0:T(4,128)S(1)} reduce(f32[4,1,24576]{2,1,0:T(1,128)S(1)} %all-to-all-done, f32[]{:T(128)} %broadcast.492), dimensions={1}, to_apply=%all_to_all.13.reduce_sub_computation | reduce | bytes 786436 | tf_op jit(solution)/shard_map/all_to_all | solution.py:118
  111.1 1.1 reshape.516
  112.2 2.2 %copy.38 = f32[16,3,16,4,32]{4,2,1,0,3:T(8,128)} copy(f32[16,3,16,4,32]{2,0,1,4,3:T(8,128)S(1)} %bitcast.176) | data formatting | bytes 786432 | tf_op jit(solution)/shard_map/all_to_all | solution.py:118
  114.5 2.0 %gather_fusion = f32[24,3,16,32]{3,2,1,0:T(8,128)S(1)} fusion(f32[64,3,16,32]{3,2,1,0:T(8,128)} %bitcast.177, s32[1024]{0:T(1024)S(1)} %pad_clamp_fusion), kind=kCustom, calls=%fused_computation | custom fusion | bytes 295008 | tf_op jit(solution)/shard_map/gather | solution.py:162
  116.5 0.3 reshape.506
  116.9 4.4 %fusion.3 = (f32[48,24,512]{2,1,0:T(8,128)S(1)}, f32[48,512]{1,0:T(8,128)S(1)}, f32[48,24,512]{2,1,0:T(8,128)}) fusion(f32[24,512]{1,0:T(8,128)S(1)} %get-tuple-element.282, f32[48]{0:T(128)S(1)} %copy-done.13, f32[24,512]{1,0:T(8,128)S(1)} %get-tuple-element.283, f32[24,512]{1,0:T(8,128)S(1)} %bitcast.181), kind=kOutput, calls=%fused_computation.9 | convolution fusion | flops 180462144 | bytes 4964544 | tf_op jit(solution)/shard_map/kj,wjc->wkc/dot_general | solution.py:132
  121.4 1.6 %fusion.70 = f32[48,512]{1,0:T(8,128)S(1)} fusion(f32[48,24,512]{2,1,0:T(8,128)S(1)} %get-tuple-element.279, f32[48,24,512]{2,1,0:T(8,128)} %get-tuple-element.281), kind=kLoop, calls=%fused_computation.163 | loop fusion | flops 49152 | bytes 294912 | tf_op jit(solution)/shard_map/exp | solution.py:134
  123.3 0.9 copy.40
  (80 shorter events, 3.9 us)
Async XLA Ops:
  2.7 26.5 %collective-permute-start.4 = (f32[8,3,16,128]{3,2,1,0:T(8,128)}, f32[8,3,16,128]{3,2,1,0:T(8,128)}, u32[]{:S(2)}, u32[]{:S(2)}) collective-permute-start(f32[8,3,16,128]{3,2,1,0:T(8,128)} %get-tuple-element.273), channel_id=1, source_target_pairs={{1,0},{2,1},{3,2},{5,4},{6,5},{7,6},{9,8},{10,9},{11,10},{13,12},{... | collective-permute-start | bytes 589832 | tf_op jit(solution)/shard_map/ppermute | solution.py:34
  5.3 25.4 %collective-permute-start.3 = (f32[8,3,16,128]{3,2,1,0:T(8,128)}, f32[8,3,16,128]{3,2,1,0:T(8,128)}, u32[]{:S(2)}, u32[]{:S(2)}) collective-permute-start(f32[8,3,16,128]{3,2,1,0:T(8,128)} %get-tuple-element.272), channel_id=1, source_target_pairs={{0,1},{1,2},{2,3},{4,5},{5,6},{6,7},{8,9},{9,10},{10,11},{12,13},{... | collective-permute-start | bytes 589832 | tf_op jit(solution)/shard_map/ppermute | solution.py:32
  9.3 22.7 %collective-permute-start.2 = (f32[8,16,3,128]{3,2,1,0:T(4,128)}, f32[8,16,3,128]{3,2,1,0:T(4,128)}, u32[]{:S(2)}, u32[]{:S(2)}) collective-permute-start(f32[8,16,3,128]{3,2,1,0:T(4,128)} %get-tuple-element.267), channel_id=1, source_target_pairs={{4,0},{8,4},{12,8},{16,12},{20,16},{24,20},{28,24},{0,28},{5,1},{9... | collective-permute-start | bytes 589832 | tf_op jit(solution)/shard_map/ppermute | solution.py:34
  9.5 22.5 %collective-permute-start.1 = (f32[8,16,3,128]{3,2,1,0:T(4,128)}, f32[8,16,3,128]{3,2,1,0:T(4,128)}, u32[]{:S(2)}, u32[]{:S(2)}) collective-permute-start(f32[8,16,3,128]{3,2,1,0:T(4,128)} %get-tuple-element.266), channel_id=1, source_target_pairs={{0,4},{4,8},{8,12},{12,16},{16,20},{20,24},{24,28},{28,0},{1,5},{5... | collective-permute-start | bytes 589832 | tf_op jit(solution)/shard_map/ppermute | solution.py:32
  14.1 1.0 copy-start
  14.1 1.1 copy-start.1
  14.1 1.1 copy-start.2
  14.1 1.2 copy-start.3
  19.1 5.2 %copy-start.11 = (s32[24]{0:T(128)S(1)}, s32[24]{0:T(128)}, u32[]{:S(2)}) copy-start(s32[24]{0:T(128)} %param.22) | copy-start | bytes 292
  19.1 5.2 %copy-start.12 = (s32[24]{0:T(128)S(1)}, s32[24]{0:T(128)}, u32[]{:S(2)}) copy-start(s32[24]{0:T(128)} %param.23) | copy-start | bytes 292
  24.6 2.1 %copy-start.6 = (f32[16,16,134]{2,1,0:T(8,128)S(1)}, f32[16,16,134]{2,1,0:T(8,128)}, u32[]{:S(2)}) copy-start(f32[16,16,134]{2,1,0:T(8,128)} %get-tuple-element.217) | copy-start | bytes 411652
  24.6 2.2 %copy-start.7 = (f32[16,16,134]{2,1,0:T(8,128)S(1)}, f32[16,16,134]{2,1,0:T(8,128)}, u32[]{:S(2)}) copy-start(f32[16,16,134]{2,1,0:T(8,128)} %get-tuple-element.221) | copy-start | bytes 411652
  26.8 1.0 copy-start.5
  26.8 1.0 copy-start.8
  28.9 0.8 copy-start.10
  28.9 1.8 %copy-start.9 = (f32[8,16,128]{2,1,0:T(8,128)S(1)}, f32[8,16,128]{2,1,0:T(8,128)}, u32[]{:S(2)}) copy-start(f32[8,16,128]{2,1,0:T(8,128)} %get-tuple-element.270) | copy-start | bytes 196612
  39.0 1.0 copy-start.4
  40.1 13.7 %collective-permute-start = (f32[16,3,16,128]{3,2,1,0:T(8,128)S(1)}, f32[16,3,16,128]{3,2,1,0:T(8,128)S(1)}, u32[]{:S(2)}, u32[]{:S(2)}) collective-permute-start(f32[16,3,16,128]{3,2,1,0:T(8,128)S(1)} %get-tuple-element.331), channel_id=1, source_target_pairs={{4,0},{8,4},{12,8},{16,12},{20,16},{24,20},{28,24},{0,28},{5,1},{9... | collective-permute-start | bytes 1179656 | tf_op jit(solution)/shard_map/while/body/eval_jaxpr/ppermute | solution.py:21
  54.0 12.9 %collective-permute-start = (f32[16,3,16,128]{3,2,1,0:T(8,128)S(1)}, f32[16,3,16,128]{3,2,1,0:T(8,128)S(1)}, u32[]{:S(2)}, u32[]{:S(2)}) collective-permute-start(f32[16,3,16,128]{3,2,1,0:T(8,128)S(1)} %get-tuple-element.331), channel_id=1, source_target_pairs={{4,0},{8,4},{12,8},{16,12},{20,16},{24,20},{28,24},{0,28},{5,1},{9... | collective-permute-start | bytes 1179656 | tf_op jit(solution)/shard_map/while/body/eval_jaxpr/ppermute | solution.py:21
  67.1 12.0 %collective-permute-start = (f32[16,3,16,128]{3,2,1,0:T(8,128)S(1)}, f32[16,3,16,128]{3,2,1,0:T(8,128)S(1)}, u32[]{:S(2)}, u32[]{:S(2)}) collective-permute-start(f32[16,3,16,128]{3,2,1,0:T(8,128)S(1)} %get-tuple-element.331), channel_id=1, source_target_pairs={{4,0},{8,4},{12,8},{16,12},{20,16},{24,20},{28,24},{0,28},{5,1},{9... | collective-permute-start | bytes 1179656 | tf_op jit(solution)/shard_map/while/body/eval_jaxpr/ppermute | solution.py:21
  79.3 11.2 %collective-permute-start = (f32[16,3,16,128]{3,2,1,0:T(8,128)S(1)}, f32[16,3,16,128]{3,2,1,0:T(8,128)S(1)}, u32[]{:S(2)}, u32[]{:S(2)}) collective-permute-start(f32[16,3,16,128]{3,2,1,0:T(8,128)S(1)} %get-tuple-element.331), channel_id=1, source_target_pairs={{4,0},{8,4},{12,8},{16,12},{20,16},{24,20},{28,24},{0,28},{5,1},{9... | collective-permute-start | bytes 1179656 | tf_op jit(solution)/shard_map/while/body/eval_jaxpr/ppermute | solution.py:21
  95.8 13.0 %all-to-all-start = ((f32[4,1,24576]{2,1,0:T(1,128)}), f32[4,1,24576]{2,1,0:T(1,128)S(1)}, u32[]{:S(2)}, u32[]{:S(2)}) async-start(f32[4,1,24576]{2,1,0:T(1,128)} %reshape.515), calls=%async_computation | async-start | bytes 786432 | tf_op jit(solution)/shard_map/all_to_all | solution.py:118
  114.4 2.4 %copy-start.13 = (f32[48]{0:T(128)S(1)}, f32[48]{0:T(128)}, u32[]{:S(2)}) copy-start(f32[48]{0:T(128)} %add_multiply_fusion) | copy-start | bytes 580
where the time goes:
time: 126 us; the launch traced here: 124 us
  waiting for transfers between devices  55.9 us (44%)
  other arithmetic  26.2 us (21%)
  local copies, waits for them, and re-layouts  18.8 us (15%)
  starting transfers between devices  16.6 us (13%)
  matrix products  5.57 us (4%)
    ppermute x4, waiting for transfers between devices, shifted(): return lax.ppermute(block, axis, route)  49.5 us
    ppermute x2, starting transfers between devices, padded_2(): lax.ppermute(tail, axis, [(i, (i + 1) % count) for i in range(ends)])  6.95 us
    unnamed x35, local copies, waits for them, and re-layouts  6.68 us
    all_to_all x1, starting transfers between devices, regroup(): lax.all_to_all(rows, 'depth', split_axis=3, concat_axis=0, tiled=True)  6.54 us
    all_to_all x1, waiting for transfers between devices, regroup(): lax.all_to_all(rows, 'depth', split_axis=3, concat_axis=0, tiled=True)  6.43 us
    dot_general x1, matrix products, emergent(): jnp.einsum('kj,wjc->wkc', earlier, dtau, precision=lax.Precision.HIGHEST)  4.39 us
    reduce_sum x3, other arithmetic, flux(): jnp.sum(moment * velocity, axis=0)  3.84 us
    ppermute x2, starting transfers between devices, padded_2(): lax.ppermute(head, axis, [((i + 1) % count, i) for i in range(ends)])  2.83 us
  transfers between devices with their start and end apart: 9, of which 5 were waited for; matrix products, arithmetic and copies ran while one was open for 14% of the time, Pallas kernels for 0%

commit v1 on v0

--- a/solution.py
+++ b/solution.py
@@ -4,6 +4,7 @@
 from jax.sharding import PartitionSpec as P
 
 W = 48
+MOST = 8
 
 
 GAMMA = 5.0 / 3.0
@@ -85,29 +86,33 @@
     return jnp.stack([dens, speed, source], axis=1)
 
 
-def rows_mask(flags):
-    return flags[:, None, None, None]
+def column_shift(level):
+    return (1732 * level + 1000) // 2000
 
 
-def shear(rows, row_shift, reach):
+def shear(rows, row_shift, depth_cells):
     cells = rows.shape[2]
-    tiles_ahead = row_shift // cells
-    offset = row_shift % cells
-
-    def advance(turn, carry):
-        piece, near, beyond = carry
-        piece = shifted(piece, "tile", -1)
-        near = jnp.where(rows_mask(tiles_ahead == turn), piece, near)
-        beyond = jnp.where(rows_mask(tiles_ahead + 1 == turn), piece, beyond)
-        return (piece, near, beyond)
-
-    start_near = jnp.where(rows_mask(tiles_ahead == 0), rows, jnp.zeros_like(rows))
-    carry = lax.fori_loop(1, reach + 2, advance, (rows, start_near, jnp.zeros_like(rows)))
-    near = carry[1]
-    beyond = carry[2]
-    joined = jnp.concatenate([near, beyond], axis=2)
+    tiles = lax.axis_size("tile")
+    slabs = lax.axis_size("depth")
+    first = [column_shift(d * depth_cells) // cells for d in range(slabs)]
+    last = [
+        (column_shift((d + 1) * depth_cells - 1) + cells - 1) // cells for d in range(slabs)
+    ]
+    count = max(high - low + 1 for low, high in zip(first, last))
+    pieces = []
+    for turn in range(count):
+        route = [
+            (((t + first[d] + turn) % tiles) * slabs + d, t * slabs + d)
+            for t in range(tiles)
+            for d in range(slabs)
+            if first[d] + turn <= last[d]
+        ]
+        pieces.append(lax.ppermute(rows, ("tile", "depth"), route))
+    joined = jnp.concatenate(pieces, axis=2)
+    lowest = lax.axis_index("depth") * depth_cells
+    offset = row_shift - column_shift(lowest) // cells * cells
     target = jnp.arange(cells, dtype=jnp.int32)
-    anchor = jnp.arange(2 * cells, dtype=jnp.int32)
+    anchor = jnp.arange(count * cells, dtype=jnp.int32)
     select = (anchor[None, None, :] == target[None, :, None] + offset[:, None, None]).astype(
         jnp.float32
     )
@@ -153,13 +158,16 @@
     along_y = jnp.pad(state, ((0, 0), (0, 0), (0, 0), (3, 3)), mode="wrap")
     new_state = state + SECTION * tendency(along_x, along_y, along_z, state)
     fields = line_fields(new_state)
-    largest = (1732 * (depth_cells * slabs - 1) + 1000) // 2000
-    reach = largest // width_cells
+    most = min(MOST, depth_cells)
     lowest = depth_at * depth_cells
-    local_level = lowest + jnp.arange(depth_cells, dtype=jnp.int32)
-    match = local_level[:, None] == levels[None, :]
-    level_shift = jnp.sum(jnp.where(match, shifts[None, :], 0), axis=1)
-    columns = regroup(shear(fields, level_shift, reach))[levels]
+    ahead = jnp.sum((levels < lowest).astype(jnp.int32))
+    position = jnp.minimum(ahead + jnp.arange(most, dtype=jnp.int32), levels.shape[0] - 1)
+    held = jnp.clip(levels[position] - lowest, 0, depth_cells - 1)
+    sheared = shear(fields[held], shifts[position], depth_cells)
+    slab = levels // depth_cells
+    before = jnp.sum((levels[None, :] < (slab * depth_cells)[:, None]).astype(jnp.int32), axis=1)
+    rank = jnp.arange(levels.shape[0], dtype=jnp.int32) - before
+    columns = regroup(sheared)[slab * most + rank]
     intensity = emergent(columns)
     return (new_state, intensity)
 

time: 126 us -> 83.8 us (0.67)
  waiting for transfers between devices: 55.9 us -> 12.8 us
  starting transfers between devices: 16.6 us -> 24.6 us
  local copies, waits for them, and re-layouts: 18.8 us -> 13.4 us
    ppermute x4 -> x3, waiting for transfers between devices: 49.5 us -> 7.49 us  [shear(): pieces.append(lax.ppermute(rows, ('tile', 'depth'), route))]
    all_to_all x1, starting transfers between devices: 6.54 us -> 12.1 us  [regroup(): lax.all_to_all(rows, 'depth', split_axis=3, concat_axis=0, tiled=True)]
    ppermute x4 -> x3, starting transfers between devices: 0.23 us -> 2.65 us  [shear(): pieces.append(lax.ppermute(rows, ('tile', 'depth'), route))]
    all_to_all x2 -> x3, local copies, waits for them, and re-layouts: 2.75 us -> 1.15 us  [regroup(): lax.all_to_all(rows, 'depth', split_axis=3, concat_axis=0, tiled=True)]
    unnamed x35, local copies, waits for them, and re-layouts: 6.68 us -> 5.16 us
    transpose x1, local copies, waits for them, and re-layouts: 2.06 us -> 0.54 us  [shear(): jnp.einsum('lcxa,lwx->lcwa', joined, select, precision=lax.Precision.HIGH...]
    gather x1 -> x4, local copies, waits for them, and re-layouts: 1.99 us -> 3 us  [the longest x2 1.77 us: per_device(): sheared = shear(fields[held], shifts[position], depth_cells)]
  transfers between devices with their start and end apart: 9 -> 8, of which waited for: 5 -> 3; matrix products, arithmetic and copies ran while one was open for 14% -> 23% of each run, Pallas kernels for 0% -> 0%
where the time goes in v1:
time: 83.8 us; the launch traced here: 83.1 us
  other arithmetic  26.4 us (32%)
  starting transfers between devices  24.6 us (29%)
  local copies, waits for them, and re-layouts  13.4 us (16%)
  waiting for transfers between devices  12.8 us (15%)
  matrix products  4.72 us (6%)
  between operations  1.15 us (1%)
    all_to_all x1, starting transfers between devices, regroup(): lax.all_to_all(rows, 'depth', split_axis=3, concat_axis=0, tiled=True)  12.1 us
    ppermute x3, waiting for transfers between devices, shear(): pieces.append(lax.ppermute(rows, ('tile', 'depth'), route))  7.49 us
    ppermute x2, starting transfers between devices, padded_2(): lax.ppermute(tail, axis, [(i, (i + 1) % count) for i in range(ends)])  6.95 us
    all_to_all x1, waiting for transfers between devices, regroup(): lax.all_to_all(rows, 'depth', split_axis=3, concat_axis=0, tiled=True)  5.33 us
    unnamed x35, local copies, waits for them, and re-layouts  5.16 us
    dot_general x1, matrix products, emergent(): jnp.einsum('kj,wjc->wkc', earlier, dtau, precision=lax.Precision.HIGHEST)  4.38 us
    reduce_sum x3, other arithmetic, flux(): jnp.sum(moment * velocity, axis=0)  3.04 us
    ppermute x2, starting transfers between devices, padded_2(): lax.ppermute(head, axis, [((i + 1) % count, i) for i in range(ends)])  2.83 us
  transfers between devices with their start and end apart: 8, of which 3 were waited for; matrix products, arithmetic and copies ran while one was open for 23% of the time, Pallas kernels for 0%

profile of v1, /device:TPU:27, one launch (start us, length us, event | category | flops | bytes accessed | tf_op | source)
XLA Modules:
  0.0 83.1 jit_solution(17729562352915992667)
XLA Ops:
  0.6 1.3 %pad_maximum_fusion.4 = f32[8,16,16,128]{3,2,1,0:T(8,128)S(1)} fusion(f32[1,16,16,128]{3,2,1,0:T(8,128)} %bitcast.166, f32[3,16,16,128]{3,2,1,0:T(8,128)} %param.18, f32[3,16,16,128]{3,2,1,0:T(8,128)} %param.17, f32[1,16,16,128]{3,2,1,0:T(8,128)} %bitcast.152), kind=kLoop, calls=%fused_computation.75 | loop fusion | flops 786432 | bytes 2097152 | tf_op jit(solution)/shard_map/concatenate | solution.py:144
  1.9 0.8 fusion.86
  2.7 2.6 %collective-permute-start.3 = (f32[8,3,16,128]{3,2,1,0:T(8,128)}, f32[8,3,16,128]{3,2,1,0:T(8,128)}, u32[]{:S(2)}, u32[]{:S(2)}) collective-permute-start(f32[8,3,16,128]{3,2,1,0:T(8,128)} %get-tuple-element.116), channel_id=1, source_target_pairs={{1,0},{2,1},{3,2},{5,4},{6,5},{7,6},{9,8},{10,9},{11,10},{13,12},{... | collective-permute-start | bytes 589832 | tf_op jit(solution)/shard_map/ppermute | solution.py:35
  5.3 3.0 %collective-permute-start.2 = (f32[8,3,16,128]{3,2,1,0:T(8,128)}, f32[8,3,16,128]{3,2,1,0:T(8,128)}, u32[]{:S(2)}, u32[]{:S(2)}) collective-permute-start(f32[8,3,16,128]{3,2,1,0:T(8,128)} %get-tuple-element.115), channel_id=1, source_target_pairs={{0,1},{1,2},{2,3},{4,5},{5,6},{6,7},{8,9},{9,10},{10,11},{12,13},{... | collective-permute-start | bytes 589832 | tf_op jit(solution)/shard_map/ppermute | solution.py:33
  8.3 0.9 %fusion.84 = (f32[8,16,3,128]{3,2,1,0:T(4,128)}, f32[8,16,3,128]{3,2,1,0:T(4,128)}) fusion(f32[8,16,16,128]{3,2,1,0:T(8,128)S(1)} %pad_maximum_fusion.4), kind=kLoop, calls=%fused_computation.197 | loop fusion | bytes 786432 | tf_op jit(solution)/shard_map/slice | solution.py:30
  9.5 3.9 %collective-permute-start = (f32[8,16,3,128]{3,2,1,0:T(4,128)}, f32[8,16,3,128]{3,2,1,0:T(4,128)}, u32[]{:S(2)}, u32[]{:S(2)}) collective-permute-start(f32[8,16,3,128]{3,2,1,0:T(4,128)} %get-tuple-element.109), channel_id=1, source_target_pairs={{0,4},{4,8},{8,12},{12,16},{16,20},{20,24},{24,28},{28,0},{1,5},{5... | collective-permute-start | bytes 589832 | tf_op jit(solution)/shard_map/ppermute | solution.py:33
  13.5 0.3 fusion.85
  13.9 0.6 copy-done.2
  14.6 1.1 %maximum_bitcast_fusion = (f32[16,16,134]{2,1,0:T(8,128)}, f32[1,16,16,134]{3,2,1,0:T(8,128)}) fusion(f32[8,16,16,3]{3,2,1,0:T(8,128)S(1)} %get-tuple-element.112, f32[8,16,16,3]{3,2,1,0:T(8,128)S(1)} %get-tuple-element.111, f32[1,16,16,128]{3,2,1,0:T(8,128)S(1)} %bitcast.167, f32[3,16,16,128]{3,2,1,0:T(8,128)S(1)} %copy-done.3, ...), kind=kLoop, calls=%fused_computation.110 | loop fusion | flops 343040 | bytes 1372160 | tf_op jit(solution)/shard_map/div | solution.py:57
  15.7 2.2 %pad_maximum_fusion = f32[8,16,16,134]{3,2,1,0:T(8,128)} fusion(f32[8,16,16,3]{3,2,1,0:T(8,128)S(1)} %get-tuple-element.112, f32[1,16,16,128]{3,2,1,0:T(8,128)S(1)} %bitcast.168, f32[3,16,16,128]{3,2,1,0:T(8,128)S(1)} %copy-done.3, f32[3,16,16,128]{3,2,1,0:T(8,128)S(1)} %copy-done.2, f32[1,16,16,128]{3,2,1,0:T(8,128)S(1)} %bitcast.154, ...), kind=kLoop, calls=%fused_computation.22 | loop fusion | flops 1372160 | bytes 2195456 | tf_op jit(solution)/shard_map/jit(_pad)/concatenate | solution.py:158
  17.9 2.7 %multiply_reduce_fusion.3 = (f32[16,16,134]{2,1,0:T(8,128)}, f32[16,16,134]{2,1,0:T(8,128)}, f32[16,16,134]{2,1,0:T(8,128)}, f32[3,16,16,134]{3,2,1,0:T(8,128)S(1)}) fusion(f32[8,16,16,134]{3,2,1,0:T(8,128)} %pad_maximum_fusion, f32[16,16,134]{2,1,0:T(8,128)} %get-tuple-element.94), kind=kLoop, calls=%fused_computation.80 | loop fusion | flops 617472 | bytes 1783808 | tf_op jit(solution)/shard_map/reduce_sum | solution.py:59
  20.6 0.9 %copy-done.6 = f32[3,16,16,134]{3,2,1,0:T(8,128)} copy-done((f32[3,16,16,134]{3,2,1,0:T(8,128)}, f32[3,16,16,134]{3,2,1,0:T(8,128)S(1)}, u32[]{:S(2)}) %copy-start.6) | copy-done | bytes 411672
  21.5 0.7 slice_bitcast_fusion
  22.2 1.2 %broadcast_multiply_fusion = (s32[24]{0:T(128)}, s32[24]{0:T(128)}, s32[]{:T(128)}) fusion(s32[24]{0:T(128)S(1)} %copy-done.1, s32[]{:T(128)S(6)} %mul.475), kind=kLoop, calls=%fused_computation.192 | loop fusion | flops 455 | bytes 296 | tf_op jit(solution)/shard_map/mul | solution.py:168
  23.4 0.6 fusion.79
  24.1 0.6 gather_fusion.1
  24.8 1.2 %gather_fusion = s32[8]{0:T(128)} fusion(s32[24]{0:T(128)S(1)} %copy-done, s32[1024]{0:T(1024)S(1)} %pad_clamp_fusion.2), kind=kCustom, calls=%fused_computation | custom fusion | bytes 96 | tf_op jit(solution)/shard_map/gather | solution.py:166
  26.0 1.4 %convert_reduce_fusion = s32[24]{0:T(128)} fusion(s32[24]{0:T(128)S(1)} %copy-done.1, s32[24]{0:T(128)} %get-tuple-element.83), kind=kLoop, calls=%fused_computation.172 | loop fusion | flops 1704 | bytes 288 | tf_op jit(solution)/shard_map/reduce_sum | solution.py:168
  27.4 2.1 %multiply_subtract_fusion = (f32[3,16,16,134]{3,2,1,0:T(8,128)S(1)}, f32[3,16,16,134]{3,2,1,0:T(8,128)S(1)}) fusion(f32[3,16,16,134]{3,2,1,0:T(8,128)} %copy-done.6, f32[8,16,16,134]{3,2,1,0:T(8,128)} %pad_maximum_fusion, f32[16,16,134]{2,1,0:T(8,128)} %bitcast.184, f32[16,16,134]{2,1,0:T(8,128)} %slice_bitcast_fusion), kind=kLoop, calls=%fused_computation.78 | loop fusion | flops 617472 | bytes 2332672 | tf_op jit(solution)/shard_map/sub | solution.py:64
  29.8 0.7 copy-done.8
  30.6 1.1 %fusion.53 = f32[1,16,16,134]{3,2,1,0:T(8,128)S(1)} fusion(f32[1,16,16,134]{3,2,1,0:T(8,128)S(1)} %copy-done.8, f32[16,16,134]{2,1,0:T(8,128)S(1)} %copy-done.11, f32[1,16,16,134]{3,2,1,0:T(8,128)S(1)} %get-tuple-element.89, f32[3,16,16,134]{3,2,1,0:T(8,128)} %copy-done.6, f32[16,16,134]{2,1,0:T(8,128)S(1)} %copy-done.10, f32[16,16,134]{2,1,0:T(8,128)S(1)} %copy-done.9), kind=kLoop, calls=%fused_computation.112 | loop fusion | flops 343040 | bytes 960512 | tf_op jit(solution)/shard_map/sub | solution.py:65
  31.7 0.3 fusion.6
  32.1 0.9 %broadcast_select_fusion = f32[8,3,16,128]{3,2,1,0:T(8,128)S(1)} fusion(f32[8,3,16,128]{3,2,1,0:T(8,128)} %collective-permute-done.3, f32[8,16,128]{2,1,0:T(8,128)S(1)} %get-tuple-element.114, pred[]{:T(512)S(6)} %eq.20), kind=kLoop, calls=%fused_computation.159 | loop fusion | flops 49152 | bytes 458753 | tf_op jit(solution)/shard_map/jit(_where)/select_n | solution.py:152
  33.0 1.0 %broadcast_select_fusion.1 = f32[8,3,16,128]{3,2,1,0:T(8,128)S(1)} fusion(f32[8,3,16,128]{3,2,1,0:T(8,128)} %collective-permute-done.2, f32[8,16,128]{2,1,0:T(8,128)S(1)} %get-tuple-element.113, pred[]{:T(512)S(6)} %eq.19), kind=kLoop, calls=%fused_computation.160 | loop fusion | flops 49152 | bytes 458753 | tf_op jit(solution)/shard_map/jit(_where)/select_n | solution.py:151
  34.4 0.8 %maximum_bitcast_fusion.1 = (f32[16,22,128]{2,1,0:T(8,128)S(1)}, f32[1,16,22,128]{3,2,1,0:T(8,128)S(1)}) fusion(f32[8,16,3,128]{3,2,1,0:T(4,128)S(1)} %collective-permute-done.1, f32[8,16,3,128]{3,2,1,0:T(4,128)} %collective-permute-done, f32[1,16,16,128]{3,2,1,0:T(8,128)S(1)} %bitcast.173, f32[3,16,16,128]{3,2,1,0:T(8,128)S(1)} %copy-done.3, ...), kind=kLoop, calls=%fused_computation.122 | loop fusion | flops 450560 | bytes 1802240 | tf_op jit(solution)/shard_map/div | solution.py:57
  35.2 1.2 %pad_maximum_fusion.1 = f32[8,16,22,128]{3,2,1,0:T(8,128)S(1)} fusion(f32[8,16,3,128]{3,2,1,0:T(4,128)S(1)} %collective-permute-done.1, f32[1,16,16,128]{3,2,1,0:T(8,128)S(1)} %bitcast.174, f32[3,16,16,128]{3,2,1,0:T(8,128)S(1)} %copy-done.3, f32[3,16,16,128]{3,2,1,0:T(8,128)S(1)} %copy-done.2, f32[1,16,16,128]{3,2,1,0:T(8,128)S(1)} %bitcast.160, ...), kind=kLoop, calls=%fused_computation.36 | loop fusion | flops 1802240 | bytes 2883584 | tf_op jit(solution)/shard_map/concatenate | solution.py:31
  37.1 0.9 %fusion.55 = (f32[3,16,22,128]{3,2,1,0:T(8,128)S(1)}, f32[1,16,22,128]{3,2,1,0:T(8,128)S(1)}) fusion(f32[3,16,22,128]{3,2,1,0:T(8,128)S(1)} %get-tuple-element.99, f32[16,22,128]{2,1,0:T(8,128)S(1)} %get-tuple-element.81, f32[16,22,128]{2,1,0:T(8,128)S(1)} %get-tuple-element.76, f32[8,16,3,128]{3,2,1,0:T(4,128)S(1)} %collective-permute-done.1, ...), kind=kLoop, calls=%fused_computation.120 | loop fusion | flops 540672 | bytes 2490368 | tf_op jit(solution)/shard_map/scatter-add | solution.py:63
  38.3 1.1 %fusion.15 = f32[8,16,22,128]{3,2,1,0:T(8,128)S(1)} fusion(f32[8,16,3,128]{3,2,1,0:T(4,128)S(1)} %collective-permute-done.1, f32[8,16,3,128]{3,2,1,0:T(4,128)} %collective-permute-done, f32[1,16,16,128]{3,2,1,0:T(8,128)S(1)} %bitcast.178, f32[3,16,16,128]{3,2,1,0:T(8,128)S(1)} %copy-done.3, f32[3,16,16,128]{3,2,1,0:T(8,128)S(1)} %copy-done.2, ...), kind=kLoop, calls=%fused_computation.27 | loop fusion | flops 5046272 | bytes 4145152 | tf_op jit(solution)/shard_map/concatenate | solution.py:66
  39.4 1.6 %fusion.33 = f32[8,16,16,128]{3,2,1,0:T(8,128)S(1)} fusion(f32[8,22,16,128]{3,2,1,0:T(8,128)S(1)} %fusion.24, f32[8,16,16,134]{3,2,1,0:T(8,128)S(1)} %fusion.6, f32[8,16,22,128]{3,2,1,0:T(8,128)S(1)} %fusion.15), kind=kLoop, calls=%fused_computation.54 | loop fusion | flops 6553600 | bytes 19922944 | tf_op jit(solution)/shard_map/neg | solution.py:71
  41.5 0.6 gather_fusion.2
  42.0 1.9 %collective-permute-start.6 = (f32[8,3,16,128]{3,2,1,0:T(8,128)S(1)}, f32[8,3,16,128]{3,2,1,0:T(8,128)S(1)}, u32[]{:S(2)}, u32[]{:S(2)}) collective-permute-start(f32[8,3,16,128]{3,2,1,0:T(8,128)S(1)} %gather_fusion.2), channel_id=1, source_target_pairs={{9,1},{14,2},{19,3},{13,5},{18,6},{23,7},{17,9},{22,10},{27,11},{2... | collective-permute-start | bytes 589832 | tf_op jit(solution)/shard_map/ppermute | solution.py:110
  44.0 0.7 collective-permute-start.4
  44.8 5.8 %collective-permute-done.6 = f32[8,3,16,128]{3,2,1,0:T(8,128)S(1)} collective-permute-done((f32[8,3,16,128]{3,2,1,0:T(8,128)S(1)}, f32[8,3,16,128]{3,2,1,0:T(8,128)S(1)}, u32[]{:S(2)}, u32[]{:S(2)}) %collective-permute-start.6) | collective-permute-done | bytes 196640 | tf_op jit(solution)/shard_map/ppermute | solution.py:110
  50.6 1.7 %collective-permute-done.5 = f32[8,3,16,128]{3,2,1,0:T(8,128)S(1)} collective-permute-done((f32[8,3,16,128]{3,2,1,0:T(8,128)S(1)}, f32[8,3,16,128]{3,2,1,0:T(8,128)S(1)}, u32[]{:S(2)}, u32[]{:S(2)}) %collective-permute-start.5) | collective-permute-done | bytes 196640 | tf_op jit(solution)/shard_map/ppermute | solution.py:110
  52.2 0.3 convolution_bitcast_fusion.1
  52.6 0.5 copy.30
  53.2 1.2 %reshape.539 = f32[4,1,12288]{2,1,0:T(1,128)} reshape(f32[128,3,8,16]{3,2,1,0:T(8,128)S(1)} %bitcast.180) | data formatting | bytes 393216
  54.4 12.1 %all-to-all-start = ((f32[4,1,12288]{2,1,0:T(1,128)}), f32[4,1,12288]{2,1,0:T(1,128)S(1)}, u32[]{:S(2)}, u32[]{:S(2)}) async-start(f32[4,1,12288]{2,1,0:T(1,128)} %reshape.539), calls=%async_computation | async-start | bytes 393216 | tf_op jit(solution)/shard_map/all_to_all | solution.py:123
  66.5 5.3 %all-to-all-done = f32[4,1,12288]{2,1,0:T(1,128)S(1)} async-done(((f32[4,1,12288]{2,1,0:T(1,128)}), f32[4,1,12288]{2,1,0:T(1,128)S(1)}, u32[]{:S(2)}, u32[]{:S(2)}) %all-to-all-start) | async-done | bytes 196640 | tf_op jit(solution)/shard_map/all_to_all | solution.py:123
  71.9 0.5 broadcast.494
  72.4 1.2 %reduce.16 = f32[4,12288]{1,0:T(4,128)S(1)} reduce(f32[4,1,12288]{2,1,0:T(1,128)S(1)} %all-to-all-done, f32[]{:T(128)} %broadcast.494), dimensions={1}, to_apply=%all_to_all.13.reduce_sub_computation | reduce | bytes 393220 | tf_op jit(solution)/shard_map/all_to_all | solution.py:123
  73.6 0.5 reshape.540
  74.1 0.6 copy.36
  74.7 0.6 gather_fusion.3
  75.3 0.3 reshape.530
  75.8 4.4 %fusion.3 = (f32[48,24,512]{2,1,0:T(8,128)S(1)}, f32[48,512]{1,0:T(8,128)S(1)}, f32[48,24,512]{2,1,0:T(8,128)}) fusion(f32[24,512]{1,0:T(8,128)S(1)} %get-tuple-element.124, f32[48]{0:T(128)S(1)} %add_multiply_fusion, f32[24,512]{1,0:T(8,128)S(1)} %get-tuple-element.125, f32[24,512]{1,0:T(8,128)S(1)} %bitcast.187), kind=kOutput, calls=%fused_computation.8 | convolution fusion | flops 180462144 | bytes 4964544 | tf_op jit(solution)/shard_map/kj,wjc->wkc/dot_general | solution.py:137
  80.3 1.6 %fusion.70 = f32[48,512]{1,0:T(8,128)S(1)} fusion(f32[48,24,512]{2,1,0:T(8,128)S(1)} %get-tuple-element.120, f32[48,24,512]{2,1,0:T(8,128)} %get-tuple-element.123), kind=kLoop, calls=%fused_computation.161 | loop fusion | flops 49152 | bytes 294912 | tf_op jit(solution)/shard_map/exp | solution.py:139
  82.2 0.9 %copy.34 = f32[48,16,32]{0,2,1:T(8,128)} copy(f32[48,16,32]{2,1,0:T(8,128)S(1)} %multiply_add_fusion.1) | data formatting | bytes 196608
  (71 shorter events, 3.4 us)
Async XLA Ops:
  0.6 24.1 %copy-start = (s32[24]{0:T(128)S(1)}, s32[24]{0:T(128)}, u32[]{:S(2)}) copy-start(s32[24]{0:T(128)} %param.20) | copy-start | bytes 292
  2.7 29.3 %collective-permute-start.3 = (f32[8,3,16,128]{3,2,1,0:T(8,128)}, f32[8,3,16,128]{3,2,1,0:T(8,128)}, u32[]{:S(2)}, u32[]{:S(2)}) collective-permute-start(f32[8,3,16,128]{3,2,1,0:T(8,128)} %get-tuple-element.116), channel_id=1, source_target_pairs={{1,0},{2,1},{3,2},{5,4},{6,5},{7,6},{9,8},{10,9},{11,10},{13,12},{... | collective-permute-start | bytes 589832 | tf_op jit(solution)/shard_map/ppermute | solution.py:35
  5.3 27.7 %collective-permute-start.2 = (f32[8,3,16,128]{3,2,1,0:T(8,128)}, f32[8,3,16,128]{3,2,1,0:T(8,128)}, u32[]{:S(2)}, u32[]{:S(2)}) collective-permute-start(f32[8,3,16,128]{3,2,1,0:T(8,128)} %get-tuple-element.115), channel_id=1, source_target_pairs={{0,1},{1,2},{2,3},{4,5},{5,6},{6,7},{8,9},{9,10},{10,11},{12,13},{... | collective-permute-start | bytes 589832 | tf_op jit(solution)/shard_map/ppermute | solution.py:33
  9.3 25.1 %collective-permute-start.1 = (f32[8,16,3,128]{3,2,1,0:T(4,128)}, f32[8,16,3,128]{3,2,1,0:T(4,128)S(1)}, u32[]{:S(2)}, u32[]{:S(2)}) collective-permute-start(f32[8,16,3,128]{3,2,1,0:T(4,128)} %get-tuple-element.110), channel_id=1, source_target_pairs={{4,0},{8,4},{12,8},{16,12},{20,16},{24,20},{28,24},{0,28},{5,1},{9... | collective-permute-start | bytes 589832 | tf_op jit(solution)/shard_map/ppermute | solution.py:35
  9.5 24.8 %collective-permute-start = (f32[8,16,3,128]{3,2,1,0:T(4,128)}, f32[8,16,3,128]{3,2,1,0:T(4,128)}, u32[]{:S(2)}, u32[]{:S(2)}) collective-permute-start(f32[8,16,3,128]{3,2,1,0:T(4,128)} %get-tuple-element.109), channel_id=1, source_target_pairs={{0,4},{4,8},{8,12},{12,16},{16,20},{20,24},{24,28},{28,0},{1,5},{5... | collective-permute-start | bytes 589832 | tf_op jit(solution)/shard_map/ppermute | solution.py:33
  13.4 1.0 %copy-start.2 = (f32[3,16,16,128]{3,2,1,0:T(8,128)S(1)}, f32[3,16,16,128]{3,2,1,0:T(8,128)}, u32[]{:S(2)}) copy-start(f32[3,16,16,128]{3,2,1,0:T(8,128)} %param.17) | copy-start | bytes 1179652
  13.5 1.1 %copy-start.3 = (f32[3,16,16,128]{3,2,1,0:T(8,128)S(1)}, f32[3,16,16,128]{3,2,1,0:T(8,128)}, u32[]{:S(2)}) copy-start(f32[3,16,16,128]{3,2,1,0:T(8,128)} %param.18) | copy-start | bytes 1179652
  13.5 1.1 %copy-start.4 = (f32[16,16,128]{2,1,0:T(8,128)S(1)}, f32[16,16,128]{2,1,0:T(8,128)}, u32[]{:S(2)}) copy-start(f32[16,16,128]{2,1,0:T(8,128)} %param.16) | copy-start | bytes 393220
  13.5 1.2 %copy-start.5 = (f32[16,16,128]{2,1,0:T(8,128)S(1)}, f32[16,16,128]{2,1,0:T(8,128)}, u32[]{:S(2)}) copy-start(f32[16,16,128]{2,1,0:T(8,128)} %param.19) | copy-start | bytes 393220
  17.9 4.3 %copy-start.1 = (s32[24]{0:T(128)S(1)}, s32[24]{0:T(128)}, u32[]{:S(2)}) copy-start(s32[24]{0:T(128)} %param.21) | copy-start | bytes 292
  20.6 0.9 %copy-start.6 = (f32[3,16,16,134]{3,2,1,0:T(8,128)}, f32[3,16,16,134]{3,2,1,0:T(8,128)S(1)}, u32[]{:S(2)}) copy-start(f32[3,16,16,134]{3,2,1,0:T(8,128)S(1)} %get-tuple-element.90) | copy-start | bytes 1234948
  27.4 2.1 %copy-start.9 = (f32[16,16,134]{2,1,0:T(8,128)S(1)}, f32[16,16,134]{2,1,0:T(8,128)}, u32[]{:S(2)}) copy-start(f32[16,16,134]{2,1,0:T(8,128)} %get-tuple-element.74) | copy-start | bytes 411652
  27.4 2.2 %copy-start.10 = (f32[16,16,134]{2,1,0:T(8,128)S(1)}, f32[16,16,134]{2,1,0:T(8,128)}, u32[]{:S(2)}) copy-start(f32[16,16,134]{2,1,0:T(8,128)} %get-tuple-element.78) | copy-start | bytes 411652
  29.5 1.0 %copy-start.8 = (f32[1,16,16,134]{3,2,1,0:T(8,128)S(1)}, f32[1,16,16,134]{3,2,1,0:T(8,128)}, u32[]{:S(2)}) copy-start(f32[1,16,16,134]{3,2,1,0:T(8,128)} %get-tuple-element.95) | copy-start | bytes 411652
  29.5 1.0 %copy-start.11 = (f32[16,16,134]{2,1,0:T(8,128)S(1)}, f32[16,16,134]{2,1,0:T(8,128)}, u32[]{:S(2)}) copy-start(f32[16,16,134]{2,1,0:T(8,128)} %get-tuple-element.75) | copy-start | bytes 411652
  29.8 1.9 %copy-start.13 = (s32[8]{0:T(128)S(1)}, s32[8]{0:T(128)}, u32[]{:S(2)}) copy-start(s32[8]{0:T(128)} %gather_fusion) | copy-start | bytes 100
  41.2 11.4 %copy-start.7 = (f32[8,16,16,128]{3,2,1,0:T(8,128)}, f32[8,16,16,128]{3,2,1,0:T(8,128)S(1)}, u32[]{:S(2)}) copy-start(f32[8,16,16,128]{3,2,1,0:T(8,128)S(1)} %multiply_add_fusion) | copy-start | bytes 3145732
  41.2 3.5 %copy-start.12 = (s32[24]{0:T(128)S(1)}, s32[24]{0:T(128)}, u32[]{:S(2)}) copy-start(s32[24]{0:T(128)} %get-tuple-element.84) | copy-start | bytes 292
  41.2 3.5 %copy-start.14 = (s32[24]{0:T(128)S(1)}, s32[24]{0:T(128)}, u32[]{:S(2)}) copy-start(s32[24]{0:T(128)} %convert_reduce_fusion) | copy-start | bytes 292
  42.0 8.5 %collective-permute-start.6 = (f32[8,3,16,128]{3,2,1,0:T(8,128)S(1)}, f32[8,3,16,128]{3,2,1,0:T(8,128)S(1)}, u32[]{:S(2)}, u32[]{:S(2)}) collective-permute-start(f32[8,3,16,128]{3,2,1,0:T(8,128)S(1)} %gather_fusion.2), channel_id=1, source_target_pairs={{9,1},{14,2},{19,3},{13,5},{18,6},{23,7},{17,9},{22,10},{27,11},{2... | collective-permute-start | bytes 589832 | tf_op jit(solution)/shard_map/ppermute | solution.py:110
  44.0 8.3 %collective-permute-start.5 = (f32[8,3,16,128]{3,2,1,0:T(8,128)S(1)}, f32[8,3,16,128]{3,2,1,0:T(8,128)S(1)}, u32[]{:S(2)}, u32[]{:S(2)}) collective-permute-start(f32[8,3,16,128]{3,2,1,0:T(8,128)S(1)} %gather_fusion.2), channel_id=1, source_target_pairs={{4,0},{5,1},{10,2},{15,3},{8,4},{9,5},{14,6},{19,7},{12,8},{13,9},... | collective-permute-start | bytes 589832 | tf_op jit(solution)/shard_map/ppermute | solution.py:110
  44.0 8.2 %collective-permute-start.4 = (f32[8,3,16,128]{3,2,1,0:T(8,128)S(1)}, f32[8,3,16,128]{3,2,1,0:T(8,128)S(1)}, u32[]{:S(2)}, u32[]{:S(2)}) collective-permute-start(f32[8,3,16,128]{3,2,1,0:T(8,128)S(1)} %gather_fusion.2), channel_id=1, source_target_pairs={{0,0},{1,1},{6,2},{11,3},{4,4},{5,5},{10,6},{15,7},{8,8},{9,9},{14... | collective-permute-start | bytes 589832 | tf_op jit(solution)/shard_map/ppermute | solution.py:110
  54.4 17.5 %all-to-all-start = ((f32[4,1,12288]{2,1,0:T(1,128)}), f32[4,1,12288]{2,1,0:T(1,128)S(1)}, u32[]{:S(2)}, u32[]{:S(2)}) async-start(f32[4,1,12288]{2,1,0:T(1,128)} %reshape.539), calls=%async_computation | async-start | bytes 393216 | tf_op jit(solution)/shard_map/all_to_all | solution.py:123
